TPU v7x, 32 devices: a whole 2x2x4 slice. The times are simulated.
32 devices in a mesh: dp: 8 (over z, x), tensor: 4 (over y, core).
Axes of the slice: x: 2, y: 2, z: 4, core: 2. Of those that a mesh axis runs over, the one named last changes fastest.
Arguments:
- hidden_in: bfloat16 [16384, 768], P('dp'), may hold values from -6 to 6
- doc_ids: int32 [16384], P('dp'), may hold values from 0 to 7, as said below
- ln1_gain: float32 [768], replicated, may hold values from 0.5 to 1.5
- ln1_bias: float32 [768], replicated, may hold values from -1.25 to 1.25
- w_qkv: bfloat16 [768, 3, 12, 64], P(None, None, 'tensor'), may hold values from -0.3125 to 0.3125
- b_qv: float32 [2, 12, 64], P(None, 'tensor'), may hold values from -1.75 to 1.75
- w_out: bfloat16 [12, 64, 768], P('tensor'), may hold values from -0.875 to 0.875
- b_out: float32 [768], replicated, may hold values from -1.25 to 1.25
- ln2_gain: float32 [768], replicated, may hold values from 0.5 to 1.5
- ln2_bias: float32 [768], replicated, may hold values from -1.25 to 1.25
- w_fc: bfloat16 [768, 3072], P(None, 'tensor'), may hold values from -0.21875 to 0.21875
- b_fc: float32 [24, 128], P('tensor'), may hold values from -1.75 to 1.75
- w_proj: bfloat16 [3072, 768], P('tensor'), may hold values from -0.109375 to 0.109375
- b_proj: float32 [768], replicated, may hold values from -1.25 to 1.25
- grad_out: bfloat16 [16384, 768], P('dp'), may hold values from -6 to 6
Outputs:
- block_out: bfloat16 [16384, 768], P('dp')
- grad_in: float32 [16384, 768], P('dp')
- grad_ln1_gain: float32 [768], P('dp')
- grad_ln1_bias: float32 [768], P('dp')
- grad_w_qkv: float32 [768, 3, 12, 64], P('dp', None, 'tensor')
- grad_b_qv: float32 [2, 12, 64], P(None, 'tensor', 'dp')
- grad_w_out: float32 [12, 64, 768], P('tensor', None, 'dp')
- grad_b_out: float32 [768], P('dp')
- grad_ln2_gain: float32 [768], P('dp')
- grad_ln2_bias: float32 [768], P('dp')
- grad_w_fc: float32 [768, 3072], P('dp', 'tensor')
- grad_b_fc: float32 [24, 128], P('tensor', 'dp')
- grad_w_proj: float32 [3072, 768], P('tensor', 'dp')
- grad_b_proj: float32 [768], P('dp')
Inputs may be any that keep to these rules, and one draw needn't show every extreme that they name: `doc_ids`: each aligned block of 2048 tokens (one index of dp) holds either 2048 // 1024 sequences of 1024 tokens or 8 sequences of 256 tokens, numbered from 0 in order; exactly half of the blocks hold the long ones.
All inputs are finite; a program needn't handle non-finite values.
Results may differ from a plain program's by a relative error of at most 0.015.
The roundings to bfloat16 on the way count: a program that leaves them out, or rounds other values in their place, can miss the bound.
Values may be sent and summed in bfloat16 or wider, within the bound.
No kernel may reach another device: no remote copies, remote signals or barrier semaphores. Data moves between devices by JAX's collectives and lax.ppermute only.
A program may use at most 192 MiB of HBM per device.

v0:
```python
import math
import jax
import jax.numpy as jnp
from jax import lax
from jax.sharding import PartitionSpec as P

EPSILON = 1e-05
MASKED = -1e30


def normalize(values):
    row_mean = jnp.mean(values, axis=-1, keepdims=True)
    centered = values - row_mean
    inv_std = lax.rsqrt(jnp.mean(centered * centered, axis=-1, keepdims=True) + EPSILON)
    return (centered * inv_std, inv_std)


def norm_back(grad_normed, normed, inv_std, gain_vec):
    scaled = grad_normed * gain_vec
    return inv_std * (
        scaled
        - jnp.mean(scaled, axis=-1, keepdims=True)
        - normed * jnp.mean(scaled * normed, axis=-1, keepdims=True)
    )


def masked_scores(queries, key_rows, row_ids, key_ids, start_row, scale_factor):
    scores = (
        jnp.einsum("qhd,khd->hqk", queries, key_rows, preferred_element_type=jnp.float32)
        * scale_factor
    )
    row_pos = start_row + jnp.arange(queries.shape[0])
    key_pos = jnp.arange(key_rows.shape[0])
    allowed = (row_pos[:, None] >= key_pos[None, :]) & (row_ids[:, None] == key_ids[None, :])
    return jnp.where(allowed[None], scores, MASKED)


def body(
    hidden_in,
    doc_ids,
    ln1_gain,
    ln1_bias,
    w_qkv,
    b_qv,
    w_out,
    b_out,
    ln2_gain,
    ln2_bias,
    w_fc,
    b_fc,
    w_proj,
    b_proj,
    grad_out,
):
    row_count, model_width = hidden_in.shape
    local_heads = w_qkv.shape[2]
    head_dim = w_qkv.shape[3]
    local_width = local_heads * head_dim
    hidden_units = w_fc.shape[1]
    scale_factor = 1.0 / math.sqrt(head_dim)
    block_rows = min(512, row_count)
    block_count = row_count // block_rows
    qkv_matrix = w_qkv.reshape(model_width, 3 * local_width)
    out_matrix = w_out.reshape(local_width, model_width)
    x_float = hidden_in.astype(jnp.float32)
    normed_one, inv_one = normalize(x_float)
    first_in = (normed_one * ln1_gain + ln1_bias).astype(jnp.bfloat16)
    projected = jnp.dot(first_in, qkv_matrix, preferred_element_type=jnp.float32).reshape(
        row_count, 3, local_heads, head_dim
    )
    queries = (projected[:, 0] + b_qv[0]).astype(jnp.bfloat16)
    key_rows = projected[:, 1].astype(jnp.bfloat16)
    value_rows = (projected[:, 2] + b_qv[1]).astype(jnp.bfloat16)
    attended_parts = []
    log_totals = []
    for block_index in range(block_count):
        start_row = block_index * block_rows
        end_row = start_row + block_rows
        scores = masked_scores(
            queries[start_row:end_row],
            key_rows[:end_row],
            doc_ids[start_row:end_row],
            doc_ids[:end_row],
            start_row,
            scale_factor,
        )
        row_max = jnp.max(scores, axis=-1, keepdims=True)
        exp_scores = jnp.exp(scores - row_max)
        row_total = jnp.sum(exp_scores, axis=-1, keepdims=True)
        weights_low = (exp_scores / row_total).astype(jnp.bfloat16)
        log_totals.append(row_max + jnp.log(row_total))
        attended_parts.append(
            jnp.einsum(
                "hqk,khd->qhd",
                weights_low,
                value_rows[:end_row],
                preferred_element_type=jnp.float32,
            )
        )
    attended = (
        jnp.concatenate(attended_parts, axis=0).reshape(row_count, local_width).astype(jnp.bfloat16)
    )
    branch_part = jnp.dot(attended, out_matrix, preferred_element_type=jnp.float32)
    branch = lax.psum(branch_part, "tensor") + b_out
    residual = x_float + branch
    normed_two, inv_two = normalize(residual)
    second_in = (normed_two * ln2_gain + ln2_bias).astype(jnp.bfloat16)
    pre_act = jnp.dot(second_in, w_fc, preferred_element_type=jnp.float32) + b_fc.reshape(
        hidden_units
    )
    act_value, gelu_back = jax.vjp(
        lambda pre_value: jax.nn.gelu(pre_value, approximate=True), pre_act
    )
    act_low = act_value.astype(jnp.bfloat16)
    mlp_part = jnp.dot(act_low, w_proj, preferred_element_type=jnp.float32)
    block_out = (
        residual + lax.psum(mlp_part.astype(jnp.bfloat16), "tensor").astype(jnp.float32) + b_proj
    )
    grad_float = grad_out.astype(jnp.float32)
    grad_w_proj = jnp.einsum("rf,rd->fd", act_low, grad_out, preferred_element_type=jnp.float32)
    grad_b_proj = jnp.sum(grad_float, axis=0)
    grad_act = jnp.einsum("rd,fd->rf", grad_out, w_proj, preferred_element_type=jnp.float32)
    grad_pre = gelu_back(grad_act)[0].astype(jnp.bfloat16)
    grad_w_fc = jnp.einsum("rd,rf->df", second_in, grad_pre, preferred_element_type=jnp.float32)
    grad_b_fc = jnp.sum(grad_pre.astype(jnp.float32), axis=0).reshape(b_fc.shape)
    grad_second_part = jnp.einsum("rf,df->rd", grad_pre, w_fc, preferred_element_type=jnp.float32)
    grad_second = lax.psum(grad_second_part, "tensor")
    grad_ln2_gain = jnp.sum(grad_second * normed_two, axis=0)
    grad_ln2_bias = jnp.sum(grad_second, axis=0)
    grad_residual = grad_float + norm_back(grad_second, normed_two, inv_two, ln2_gain)
    grad_branch = grad_residual.astype(jnp.bfloat16)
    grad_b_out = jnp.sum(grad_branch.astype(jnp.float32), axis=0)
    grad_w_out = jnp.einsum(
        "rc,rd->cd", attended, grad_branch, preferred_element_type=jnp.float32
    ).reshape(w_out.shape)
    grad_attended = (
        jnp.einsum("rd,cd->rc", grad_branch, out_matrix, preferred_element_type=jnp.float32)
        .astype(jnp.bfloat16)
        .reshape(row_count, local_heads, head_dim)
    )
    grad_query_parts = []
    grad_keys = jnp.zeros((row_count, local_heads, head_dim), jnp.float32)
    grad_values = jnp.zeros((row_count, local_heads, head_dim), jnp.float32)
    for block_index in range(block_count):
        start_row = block_index * block_rows
        end_row = start_row + block_rows
        block_queries = queries[start_row:end_row]
        scores = masked_scores(
            block_queries,
            key_rows[:end_row],
            doc_ids[start_row:end_row],
            doc_ids[:end_row],
            start_row,
            scale_factor,
        )
        attn_weights = jnp.exp(scores - log_totals[block_index])
        weights_low = attn_weights.astype(jnp.bfloat16)
        grad_rows = grad_attended[start_row:end_row]
        grad_weights = jnp.einsum(
            "qhd,khd->hqk", grad_rows, value_rows[:end_row], preferred_element_type=jnp.float32
        )
        row_delta = jnp.sum(attn_weights * grad_weights, axis=-1, keepdims=True)
        grad_scores = (attn_weights * (grad_weights - row_delta)).astype(jnp.bfloat16)
        grad_query_parts.append(
            jnp.einsum(
                "hqk,khd->qhd", grad_scores, key_rows[:end_row], preferred_element_type=jnp.float32
            )
            * scale_factor
        )
        grad_keys = grad_keys.at[:end_row].add(
            jnp.einsum(
                "hqk,qhd->khd", grad_scores, block_queries, preferred_element_type=jnp.float32
            )
            * scale_factor
        )
        grad_values = grad_values.at[:end_row].add(
            jnp.einsum("hqk,qhd->khd", weights_low, grad_rows, preferred_element_type=jnp.float32)
        )
    grad_queries = jnp.concatenate(grad_query_parts, axis=0)
    grad_mixed = jnp.stack([grad_queries, grad_keys, grad_values], axis=1).astype(jnp.bfloat16)
    grad_flat = grad_mixed.reshape(row_count, 3 * local_width)
    grad_w_qkv = jnp.einsum(
        "rd,rc->dc", first_in, grad_flat, preferred_element_type=jnp.float32
    ).reshape(w_qkv.shape)
    grad_b_qv = jnp.stack(
        [
            jnp.sum(grad_mixed[:, 0].astype(jnp.float32), axis=0),
            jnp.sum(grad_mixed[:, 2].astype(jnp.float32), axis=0),
        ],
        axis=0,
    )
    grad_first_part = jnp.einsum(
        "rc,dc->rd", grad_flat, qkv_matrix, preferred_element_type=jnp.float32
    )
    grad_first = lax.psum(grad_first_part.astype(jnp.bfloat16), "tensor").astype(jnp.float32)
    grad_ln1_gain = jnp.sum(grad_first * normed_one, axis=0)
    grad_ln1_bias = jnp.sum(grad_first, axis=0)
    grad_in = grad_residual + norm_back(grad_first, normed_one, inv_one, ln1_gain)
    shares = (
        lax.psum_scatter(grad_ln1_gain, "dp", scatter_dimension=0, tiled=True),
        lax.psum_scatter(grad_ln1_bias, "dp", scatter_dimension=0, tiled=True),
        lax.psum_scatter(grad_w_qkv, "dp", scatter_dimension=0, tiled=True),
        lax.psum_scatter(grad_b_qv, "dp", scatter_dimension=2, tiled=True),
        lax.psum_scatter(grad_w_out, "dp", scatter_dimension=2, tiled=True),
        lax.psum_scatter(grad_b_out, "dp", scatter_dimension=0, tiled=True),
        lax.psum_scatter(grad_ln2_gain, "dp", scatter_dimension=0, tiled=True),
        lax.psum_scatter(grad_ln2_bias, "dp", scatter_dimension=0, tiled=True),
        lax.psum_scatter(grad_w_fc, "dp", scatter_dimension=0, tiled=True),
        lax.psum_scatter(grad_b_fc, "dp", scatter_dimension=1, tiled=True),
        lax.psum_scatter(grad_w_proj, "dp", scatter_dimension=1, tiled=True),
        lax.psum_scatter(grad_b_proj, "dp", scatter_dimension=0, tiled=True),
    )
    return (
        block_out.astype(jnp.bfloat16),
        grad_in,
        shares[0],
        shares[1],
        shares[2],
        shares[3],
        shares[4],
        shares[5],
        shares[6],
        shares[7],
        shares[8],
        shares[9],
        shares[10],
        shares[11],
    )


def solution(mesh):
    in_specs = (
        P("dp", None),
        P("dp"),
        P(),
        P(),
        P(None, None, "tensor", None),
        P(None, "tensor", None),
        P("tensor", None, None),
        P(),
        P(),
        P(),
        P(None, "tensor"),
        P("tensor", None),
        P("tensor", None),
        P(),
        P("dp", None),
    )
    out_specs = (
        P("dp", None),
        P("dp", None),
        P("dp"),
        P("dp"),
        P("dp", None, "tensor", None),
        P(None, "tensor", "dp"),
        P("tensor", None, "dp"),
        P("dp"),
        P("dp"),
        P("dp"),
        P("dp", "tensor"),
        P("tensor", "dp"),
        P("tensor", "dp"),
        P("dp"),
    )
    return jax.shard_map(body, mesh=mesh, in_specs=in_specs, out_specs=out_specs, check_vma=False)
```

profile of v0, /device:TPU:0, one launch (start us, length us, event | category | flops | bytes accessed | tf_op | source)
XLA Modules:
  0.0 799.8 jit_solution(18134782078654954278)
XLA Ops:
  8.2 1.1 fusion.135
  9.3 2.4 convert_reduce_fusion.1
  11.7 2.9 fusion.16
  15.5 2.3 fusion.136
  18.8 1.5 fusion.139
  21.4 1.5 fusion.30
  22.9 1.5 fusion.103
  25.2 2.3 fusion.138
  27.5 1.4 fusion.5
  28.9 2.3 fusion.94
  31.2 1.0 fusion.36
  32.2 3.8 fusion.137
  36.1 1.9 fusion
  38.0 2.6 copy-done.2
  40.6 3.1 fusion.104
  43.7 3.7 convolution_bitcast_fusion
  47.9 122.0 %all-reduce.15.cloned.1.call-done = f32[2048,768]{1,0:T(8,128)} async-done(((f32[2048,768]{1,0:T(8,128)}), f32[2048,768]{1,0:T(8,128)}) %all-reduce.15.cloned.1.call-update) | async-done | bytes 6291472 | tf_op jit(solution)/shard_map/psum | solution.py:104
  170.0 4.6 fusion.132
  175.5 1.1 add_convert_fusion.1
  177.6 2.6 fusion.141
  180.7 7.7 convert_reduce_fusion.3
  188.4 1.6 copy-done.44
  190.0 4.5 fusion.142
  195.4 6.2 convolution_convert_fusion
  201.8 112.7 %all-reduce.17.cloned.1.call-done = f32[2048,768]{1,0:T(8,128)} async-done(((f32[2048,768]{1,0:T(8,128)}), f32[2048,768]{1,0:T(8,128)}) %all-reduce.17.cloned.1.call-update) | async-done | bytes 6291472 | tf_op jit(solution)/shard_map/psum | solution.py:127
  314.5 6.6 multiply_reduce_fusion.2
  321.8 5.8 convert_reduce_fusion.4
  327.7 2.1 fusion.40
  329.8 1.2 convolution_convert_fusion.1
  332.5 2.3 multiply_reduce_fusion.7
  335.0 4.2 multiply_reduce_fusion.3
  339.1 1.2 fusion.88
  341.1 5.7 multiply_reduce_fusion.1
  346.8 2.1 fusion.61
  349.1 6.4 multiply_reduce_fusion
  355.6 3.1 fusion.67
  358.7 2.9 multiply_convert_fusion.4
  362.8 3.5 multiply_convert_fusion.2
  366.3 2.1 fusion.101
  369.2 5.4 multiply_convert_fusion.1
  374.6 1.5 fusion.105
  377.1 6.3 multiply_convert_fusion
  383.4 2.0 fusion.99
  385.5 2.1 fusion.57
  387.6 1.1 fusion.102
  389.4 1.7 reshape.591
  392.2 1.4 maximum_convert_fusion
  393.6 5.5 bitcast_convert_fusion
  399.8 5.5 fusion.71
  405.3 2.8 copy.57
  408.2 6.9 fusion.143
  415.2 6.9 fusion.144
  424.1 1.4 copy.56
  425.8 29.0 %reduce-scatter.19.cloned.1.call-done = f32[96,192]{1,0:T(8,128)} async-done(((f32[768,192]{1,0:T(8,128)}), f32[96,192]{1,0:T(8,128)}) %reduce-scatter.19.cloned.1.call-update) | async-done | bytes 73744
  456.5 119.1 %all-reduce.19.cloned.1.call-done = (bf16[2048,768]{1,0:T(8,128)(2,1)}, bf16[2048,768]{1,0:T(8,128)(2,1)}) async-done(((bf16[2048,768]{1,0:T(8,128)(2,1)}, bf16[2048,768]{1,0:T(8,128)(2,1)}), (bf16[2048,768]{1,0:T(8,128)(2,1)}, bf16[2048,768]{1,0:T(8,128)(2,1)})) %all-reduce.19.cloned.1.call-update) | async-done | bytes 6291472 | tf_op jit(solution)/shard_map/psum | solution.py:117
  575.6 5.2 fusion.25
  580.9 38.1 %all-reduce.9 = (f32[768]{0:T(1024)S(1)}, f32[768]{0:T(1024)S(1)}, f32[2,3,64]{2,1,0:T(4,128)S(1)}, f32[768]{0:T(1024)S(1)}, f32[768]{0:T(1024)S(1)}, /*index=5*/f32[768]{0:T(1024)S(1)}, f32[768]{0:T(1024)S(1)}) all-reduce(f32[768]{0:T(1024)S(1)} %get-tuple-element.156, ...), channel_id=2, replica_groups=mesh['dp'=8,'tensor'=4] {'dp'}, use_global_device_ids=true, to_apply=%region_25.26.clone | all-reduce | flops 4992 | bytes 39936
  623.2 6.4 add_convert_fusion
  629.7 1.5 copy-done.12
  631.2 4.2 fusion.15
  635.4 11.5 %reduce-scatter.17.cloned.1.call-done = f32[96,576]{1,0:T(8,128)} async-done(((f32[768,576]{1,0:T(8,128)}), f32[96,576]{1,0:T(8,128)}) %reduce-scatter.17.cloned.1.call-update) | async-done | bytes 221200
  647.0 1.8 copy.58
  648.8 70.8 %reduce-scatter.13.cloned.1.call-done = f32[96,768]{1,0:T(8,128)} async-done(((f32[768,768]{1,0:T(8,128)}), f32[96,768]{1,0:T(8,128)}) %reduce-scatter.13.cloned.1.call-update) | async-done | bytes 294928 | tf_op jit(solution)/shard_map/reduce_scatter | solution.py:208
  719.6 72.9 %reduce-scatter.15.cloned.1.call-done = f32[768,96]{0,1:T(8,128)} async-done(((f32[768,768]{0,1:T(8,128)}), f32[768,96]{0,1:T(8,128)}) %reduce-scatter.15.cloned.1.call-update) | async-done | bytes 294928 | tf_op jit(solution)/shard_map/reduce_scatter | solution.py:210
  (182 shorter events, 24.0 us)
Async XLA Ops:
  7.2 173.1 %copy-start = (bf16[768,768]{1,0:T(8,128)(2,1)S(1)}, bf16[768,768]{1,0:T(8,128)(2,1)}, u32[]{:S(2)}) copy-start(bf16[768,768]{1,0:T(8,128)(2,1)} %param.47) | copy-start | bytes 3538948
  7.2 7.7 slice-start.12
  7.2 8.2 %copy-start.33 = (f32[768]{0:T(1024)S(1)}, f32[768]{0:T(1024)}, u32[]{:S(2)}) copy-start(f32[768]{0:T(1024)} %param.37) | copy-start | bytes 9220
  7.2 8.2 %copy-start.39 = (bf16[768,3,3,64]{0,3,2,1:T(8,128)(2,1)S(1)}, bf16[768,3,3,64]{0,3,2,1:T(8,128)(2,1)}, u32[]{:S(2)}) copy-start(bf16[768,3,3,64]{0,3,2,1:T(8,128)(2,1)} %param.39) | copy-start | bytes 2654212
  7.2 8.2 %copy-start.41 = (f32[768]{0:T(1024)S(1)}, f32[768]{0:T(1024)}, u32[]{:S(2)}) copy-start(f32[768]{0:T(1024)} %param.38) | copy-start | bytes 9220
  7.2 162.7 %all-reduce.15.cloned.1.call-start = ((), (), s32[]{:S(2)}) async-start(), calls=%async_computation.5 | async-start | bytes 12582912 | tf_op jit(solution)/shard_map/psum | solution.py:104
  7.3 8.2 %copy-start.7 = (bf16[2048,768]{1,0:T(8,128)(2,1)S(1)}, bf16[2048,768]{1,0:T(8,128)(2,1)}, u32[]{:S(2)}) copy-start(bf16[2048,768]{1,0:T(8,128)(2,1)} %param.35) | copy-start | bytes 9437188
  11.7 6.1 copy-start.23
  14.7 3.1 copy-start.26
  17.8 7.4 copy-start.20
  18.0 14.2 %copy-start.13 = (bf16[2048,3,64]{0,2,1:T(8,128)(2,1)}, bf16[2048,3,64]{0,2,1:T(8,128)(2,1)S(1)}, u32[]{:S(2)}) copy-start(bf16[2048,3,64]{0,2,1:T(8,128)(2,1)S(1)} %get-tuple-element.180) | copy-start | bytes 2359300
  18.8 2.6 copy-start.9
  20.3 2.6 copy-start.5
  22.9 1.5 copy-start.25
  27.5 3.7 copy-start.4
  36.1 4.5 copy-start.2
  40.6 3.1 copy-start.22
  43.7 126.2 %copy-start.37 = (f32[768]{0:T(1024)S(1)}, f32[768]{0:T(1024)}, u32[]{:S(2)}) copy-start(f32[768]{0:T(1024)} %param.42) | copy-start | bytes 9220
  47.5 267.0 %all-reduce.17.cloned.1.call-start = ((), (), s32[]{:S(2)}) async-start(), calls=%async_computation.6 | async-start | bytes 12582912 | tf_op jit(solution)/shard_map/psum | solution.py:127
  174.6 2.7 copy-start.3
  174.6 0.9 copy-start.28
  174.6 0.9 copy-start.36
  175.5 2.2 copy-start.38
  177.6 2.6 copy-start.17
  177.6 3.0 copy-start.18
  177.6 3.0 copy-start.40
  188.4 1.6 copy-start.44
  194.5 229.6 %reduce-scatter.21.cloned.1.call-start = ((), (), s32[]{:S(2)}) async-start(), calls=%async_computation.11 | async-start | bytes 73728
  201.6 253.1 %reduce-scatter.19.cloned.1.call-start = ((), (), s32[]{:S(2)}) async-start(), calls=%async_computation.10 | async-start | bytes 884736
  314.5 6.6 copy-start.11
  314.5 7.4 copy-start.19
  327.7 3.3 copy-start.6
  329.8 2.1 copy-start.10
  331.1 3.9 slice-start.6
  332.5 2.5 slice-start.7
  335.0 5.4 slice-start.3
  335.0 5.8 slice-start.4
  339.1 1.9 slice-start.5
  341.1 7.8 slice-start
  341.1 7.8 slice-start.1
  346.8 2.3 slice-start.2
  358.7 2.9 copy-start.14
  358.7 3.7 slice-start.8
  358.7 4.1 slice-start.9
  369.2 5.4 copy-start.21
  385.5 3.2 copy-start.15
  387.6 4.6 copy-start.16
  391.1 184.6 %all-reduce.19.cloned.1.call-start = ((), (), s32[]{:S(2)}) async-start(), calls=%async_computation.12 | async-start | bytes 12582912 | tf_op jit(solution)/shard_map/psum | solution.py:117
  399.1 0.7 copy-start.34
  399.1 0.7 copy-start.42
  399.1 247.9 %reduce-scatter.17.cloned.1.call-start = ((), (), s32[]{:S(2)}) async-start(), calls=%async_computation.9 | async-start | bytes 2211840
  408.1 311.4 %reduce-scatter.13.cloned.1.call-start = ((), (), s32[]{:S(2)}) async-start(), calls=%async_computation.7 | async-start | bytes 2654208 | tf_op jit(solution)/shard_map/reduce_scatter | solution.py:208
  415.1 7.0 copy-start.43
  415.2 377.4 %reduce-scatter.15.cloned.1.call-start = ((), (), s32[]{:S(2)}) async-start(), calls=%async_computation.8 | async-start | bytes 2654208 | tf_op jit(solution)/shard_map/reduce_scatter | solution.py:210
  422.1 158.7 %copy-start.29 = (f32[768]{0:T(1024)S(1)}, f32[768]{0:T(1024)}, u32[]{:S(2)}) copy-start(f32[768]{0:T(1024)} %get-tuple-element.154) | copy-start | bytes 9220
  422.1 158.7 %copy-start.30 = (f32[768]{0:T(1024)S(1)}, f32[768]{0:T(1024)}, u32[]{:S(2)}) copy-start(f32[768]{0:T(1024)} %get-tuple-element.159) | copy-start | bytes 9220
  422.1 158.7 %copy-start.31 = (f32[768]{0:T(1024)S(1)}, f32[768]{0:T(1024)}, u32[]{:S(2)}) copy-start(f32[768]{0:T(1024)} %get-tuple-element.175) | copy-start | bytes 9220
  422.1 158.7 %copy-start.32 = (f32[768]{0:T(1024)S(1)}, f32[768]{0:T(1024)}, u32[]{:S(2)}) copy-start(f32[768]{0:T(1024)} %get-tuple-element.182) | copy-start | bytes 9220
  575.6 54.0 %slice-start.10 = ((s8[6291456]{0:T(1024)(128)(4,1)}), s8[2097152]{0:T(1024)(128)(4,1)S(1)}, s32[]{:S(2)}) async-start(s8[6291456]{0:T(1024)(128)(4,1)} %bitcast.204), calls=%async_computation.23 | async-start | bytes 4194304
  623.2 6.5 slice-start.11
  623.2 6.5 copy-start.8
  623.2 8.0 %copy-start.12 = (bf16[2048,768]{1,0:T(8,128)(2,1)S(1)}, bf16[2048,768]{1,0:T(8,128)(2,1)}, u32[]{:S(2)}) copy-start(bf16[2048,768]{1,0:T(8,128)(2,1)} %get-tuple-element.172) | copy-start | bytes 9437188
  623.2 8.0 %copy-start.35 = (f32[768]{0:T(1024)S(1)}, f32[768]{0:T(1024)}, u32[]{:S(2)}) copy-start(f32[768]{0:T(1024)} %param.37) | copy-start | bytes 9220
  623.2 169.3 %copy-start.1 = (bf16[768,768]{1,0:T(8,128)(2,1)S(1)}, bf16[768,768]{1,0:T(8,128)(2,1)}, u32[]{:S(2)}) copy-start(bf16[768,768]{1,0:T(8,128)(2,1)} %param.47) | copy-start | bytes 3538948
  (2 other events, 1.4 us)
Sparse Core Ops, SparseCore 0:
  47.6 122.2 all-reduce.14
  194.7 119.7 all-reduce.16
  318.5 62.7 reduce-scatter.20
  391.2 63.4 reduce-scatter.18
  457.0 118.6 all-reduce.18
  579.0 67.9 reduce-scatter.16
  651.0 68.4 reduce-scatter.12
  723.6 68.8 reduce-scatter.14
where the time goes:
time: 809 us; the launch traced here: 800 us
  waiting for transfers between devices  538 us (67%)
  matrix products  108 us (13%)
  other arithmetic  70 us (9%)
  blocking collectives  38.1 us (5%)
  local copies, waits for them, and re-layouts  27.9 us (3%)
  between operations  16.8 us (2%)
    psum x1, waiting for transfers between devices, body(): branch = lax.psum(branch_part, 'tensor') + b_out  122 us
    psum x1, waiting for transfers between devices, body(): lax.psum(mlp_part.astype(jnp.bfloat16), 'tensor').astype(jnp.float32)  119 us
    psum x1, waiting for transfers between devices, body(): grad_second = lax.psum(grad_second_part, 'tensor')  113 us
    reduce_scatter x1, waiting for transfers between devices, body(): lax.psum_scatter(grad_w_proj, 'dp', scatter_dimension=1, tiled=True)  72.9 us
    reduce_scatter x1, waiting for transfers between devices, body(): lax.psum_scatter(grad_w_fc, 'dp', scatter_dimension=0, tiled=True)  70.8 us
    unnamed x11, waiting for transfers between devices  40.6 us
    unnamed x1, blocking collectives  38.1 us
    unnamed x132, local copies, waits for them, and re-layouts  26.4 us
  transfers between devices with their start and end apart: 8, of which 7 were waited for; matrix products, arithmetic and copies ran while one was open for 17% of the time, Pallas kernels for 0%

commit v1 on v0

--- a/solution.py
+++ b/solution.py
@@ -6,6 +6,11 @@
 
 EPSILON = 1e-05
 MASKED = -1e30
+
+
+def add_all(block, mesh_axis):
+    shards = lax.all_gather(block, mesh_axis)
+    return jnp.sum(shards, axis=0)
 
 
 def normalize(values):
@@ -114,7 +119,7 @@
     act_low = act_value.astype(jnp.bfloat16)
     mlp_part = jnp.dot(act_low, w_proj, preferred_element_type=jnp.float32)
     block_out = (
-        residual + lax.psum(mlp_part.astype(jnp.bfloat16), "tensor").astype(jnp.float32) + b_proj
+        residual + add_all(mlp_part.astype(jnp.bfloat16), "tensor").astype(jnp.float32) + b_proj
     )
     grad_float = grad_out.astype(jnp.float32)
     grad_w_proj = jnp.einsum("rf,rd->fd", act_low, grad_out, preferred_element_type=jnp.float32)

time: 809 us -> 849 us (1.049)
  waiting for transfers between devices: 538 us -> 571 us
  other arithmetic: 70 us -> 80.3 us
    all_gather x0 -> x1, waiting for transfers between devices: none -> 78 us  [add_all(): shards = lax.all_gather(block, mesh_axis)]
    psum x1, waiting for transfers between devices: 119 us -> 68 us  [body(): lax.psum(grad_first_part.astype(jnp.bfloat16), 'tensor').astype(jnp.float32)]
    reduce_sum x0 -> x1, other arithmetic: none -> 8.96 us  [add_all(): return jnp.sum(shards, axis=0)]
    unnamed x11 -> x12, waiting for transfers between devices: 40.6 us -> 46.7 us
    unnamed x132 -> x120, local copies, waits for them, and re-layouts: 26.4 us -> 23.8 us
  transfers between devices with their start and end apart: 8 -> 9, of which waited for: 7 -> 8; matrix products, arithmetic and copies ran while one was open for 17% -> 18% of each run, Pallas kernels for 0% -> 0%
where the time goes in v1:
time: 849 us; the launch traced here: 839 us
  waiting for transfers between devices  571 us (67%)
  matrix products  108 us (13%)
  other arithmetic  80.3 us (9%)
  blocking collectives  37.5 us (4%)
  local copies, waits for them, and re-layouts  25.3 us (3%)
  between operations  16.3 us (2%)
    psum x1, waiting for transfers between devices, body(): branch = lax.psum(branch_part, 'tensor') + b_out  122 us
    psum x1, waiting for transfers between devices, body(): grad_second = lax.psum(grad_second_part, 'tensor')  112 us
    all_gather x1, waiting for transfers between devices, add_all(): shards = lax.all_gather(block, mesh_axis)  78 us
    reduce_scatter x1, waiting for transfers between devices, body(): lax.psum_scatter(grad_w_proj, 'dp', scatter_dimension=1, tiled=True)  72.9 us
    reduce_scatter x1, waiting for transfers between devices, body(): lax.psum_scatter(grad_w_fc, 'dp', scatter_dimension=0, tiled=True)  70.9 us
    psum x1, waiting for transfers between devices, body(): lax.psum(grad_first_part.astype(jnp.bfloat16), 'tensor').astype(jnp.float32)  68 us
    unnamed x12, waiting for transfers between devices  46.7 us
    unnamed x1, blocking collectives  37.5 us
  transfers between devices with their start and end apart: 9, of which 8 were waited for; matrix products, arithmetic and copies ran while one was open for 18% of the time, Pallas kernels for 0%

profile of v1, /device:TPU:0, one launch (start us, length us, event | category | flops | bytes accessed | tf_op | source)
XLA Modules:
  0.0 839.2 jit_solution(11356313275690501617)
XLA Ops:
  8.2 1.1 fusion.135
  9.3 2.4 convert_reduce_fusion.1
  11.7 2.9 fusion.16
  15.5 2.3 fusion.136
  18.8 1.4 fusion.139
  21.4 1.5 fusion.30
  22.9 1.5 fusion.103
  25.2 2.3 fusion.138
  27.5 1.4 fusion.5
  28.9 2.3 fusion.94
  32.3 3.8 fusion.137
  36.2 1.9 fusion
  38.1 2.7 copy-done.2
  40.7 3.1 fusion.104
  43.8 3.7 convolution_bitcast_fusion
  48.2 121.9 %all-reduce.14.cloned.1.call-done = f32[2048,768]{1,0:T(8,128)} async-done(((f32[2048,768]{1,0:T(8,128)}), f32[2048,768]{1,0:T(8,128)}) %all-reduce.14.cloned.1.call-update) | async-done | bytes 6291472 | tf_op jit(solution)/shard_map/psum | solution.py:109
  170.1 4.6 fusion.132
  175.6 1.1 add_convert_fusion.1
  177.7 2.6 fusion.141
  180.8 7.8 convert_reduce_fusion.3
  188.6 1.6 copy-done.40
  190.2 4.5 fusion.142
  194.8 6.5 convolution_convert_fusion
  202.4 112.3 %all-reduce.16.cloned.1.call-done = f32[2048,768]{1,0:T(8,128)} async-done(((f32[2048,768]{1,0:T(8,128)}), f32[2048,768]{1,0:T(8,128)}) %all-reduce.16.cloned.1.call-update) | async-done | bytes 6291472 | tf_op jit(solution)/shard_map/psum | solution.py:132
  314.7 6.5 multiply_reduce_fusion.2
  321.2 78.0 %all-gather.3.cloned.1.call-done = bf16[8192,768]{1,0:T(8,128)(2,1)} async-done(((bf16[2048,768]{1,0:T(8,128)(2,1)}), bf16[8192,768]{1,0:T(8,128)(2,1)}) %all-gather.3.cloned.1.call-update) | async-done | bytes 12582928 | tf_op jit(solution)/shard_map/all_gather | solution.py:12
  399.1 9.0 %reduce_sum.245 = bf16[2048,768]{1,0:T(8,128)(2,1)} reduce(bf16[4,2048,768]{2,1,0:T(8,128)(2,1)} %bitcast.205, bf16[]{:T(256)} %constant.241.clone.1), dimensions={0}, to_apply=%region_13.14 | reduce | flops 4718592 | bytes 15728642 | tf_op jit(solution)/shard_map/reduce_sum | solution.py:13
  408.1 10.4 %convert_reduce_fusion.4 = (f32[768]{0:T(1024)}, f32[2048,768]{1,0:T(8,128)S(1)}, bf16[2048,768]{1,0:T(8,128)(2,1)}, f32[768]{0:T(1024)}) fusion(f32[2048]{0:T(1024)S(1)} %broadcast_multiply_fusion.2, f32[2048,768]{1,0:T(8,128)} %copy-done.3, f32[2048]{0:T(1024)S(1)} %broadcast_multiply_fusion.4, f32[2048]{0:T(1024)S(1)} %broadcast_multiply_fusion.3, ...), kind=kLoop, calls=%fused_computation.52 | loop fusion | flops 26737152 | bytes 28356608 | tf_op jit(solution)/shard_map/reduce_sum | solution.py:137
  418.5 2.3 fusion.40
  420.8 1.2 convolution_convert_fusion.1
  423.3 2.3 multiply_reduce_fusion.7
  425.9 4.2 multiply_reduce_fusion.3
  430.0 1.2 fusion.88
  432.0 5.7 multiply_reduce_fusion.1
  437.7 2.1 fusion.61
  440.1 6.5 multiply_reduce_fusion
  446.5 3.1 fusion.67
  449.6 2.9 multiply_convert_fusion.4
  453.6 3.5 multiply_convert_fusion.2
  457.2 2.1 fusion.101
  460.0 5.4 multiply_convert_fusion.1
  465.5 1.5 fusion.105
  468.0 6.3 multiply_convert_fusion
  474.3 2.0 fusion.99
  476.3 2.1 fusion.57
  478.4 1.1 fusion.102
  479.5 1.1 copy.53
  480.6 1.8 reshape.592
  483.4 1.4 maximum_convert_fusion
  484.9 5.2 bitcast_convert_fusion
  490.2 5.5 fusion.71
  495.7 2.8 copy.57
  498.6 6.9 fusion.143
  505.6 7.0 fusion.144
  514.6 1.4 copy.56
  516.3 29.5 %reduce-scatter.19.cloned.1.call-done = f32[96,192]{1,0:T(8,128)} async-done(((f32[768,192]{1,0:T(8,128)}), f32[96,192]{1,0:T(8,128)}) %reduce-scatter.19.cloned.1.call-update) | async-done | bytes 73744
  547.6 68.0 %all-reduce.18.cloned.1.call-done = bf16[2048,768]{1,0:T(8,128)(2,1)} async-done(((bf16[2048,768]{1,0:T(8,128)(2,1)}), bf16[2048,768]{1,0:T(8,128)(2,1)}) %all-reduce.18.cloned.1.call-update) | async-done | bytes 3145744 | tf_op jit(solution)/shard_map/psum | solution.py:200
  615.5 5.2 fusion.25
  620.8 37.5 %all-reduce.9 = (f32[768]{0:T(1024)S(1)}, f32[768]{0:T(1024)S(1)}, f32[2,3,64]{2,1,0:T(4,128)S(1)}, f32[768]{0:T(1024)S(1)}, f32[768]{0:T(1024)S(1)}, /*index=5*/f32[768]{0:T(1024)S(1)}, f32[768]{0:T(1024)S(1)}) all-reduce(f32[768]{0:T(1024)S(1)} %get-tuple-element.156, ...), channel_id=3, replica_groups=mesh['dp'=8,'tensor'=4] {'dp'}, use_global_device_ids=true, to_apply=%region_25.26.clone | all-reduce | flops 4992 | bytes 39936
  662.4 7.5 fusion.15
  670.0 17.0 %reduce-scatter.17.cloned.1.call-done = f32[96,576]{1,0:T(8,128)} async-done(((f32[768,576]{1,0:T(8,128)}), f32[96,576]{1,0:T(8,128)}) %reduce-scatter.17.cloned.1.call-update) | async-done | bytes 221200
  687.0 1.8 copy.58
  688.8 70.9 %reduce-scatter.13.cloned.1.call-done = f32[96,768]{1,0:T(8,128)} async-done(((f32[768,768]{1,0:T(8,128)}), f32[96,768]{1,0:T(8,128)}) %reduce-scatter.13.cloned.1.call-update) | async-done | bytes 294928 | tf_op jit(solution)/shard_map/reduce_scatter | solution.py:213
  759.6 72.9 %reduce-scatter.15.cloned.1.call-done = f32[768,96]{0,1:T(8,128)} async-done(((f32[768,768]{0,1:T(8,128)}), f32[768,96]{0,1:T(8,128)}) %reduce-scatter.15.cloned.1.call-update) | async-done | bytes 294928 | tf_op jit(solution)/shard_map/reduce_scatter | solution.py:215
  (172 shorter events, 23.0 us)
Async XLA Ops:
  7.2 173.2 %copy-start = (bf16[768,768]{1,0:T(8,128)(2,1)S(1)}, bf16[768,768]{1,0:T(8,128)(2,1)}, u32[]{:S(2)}) copy-start(bf16[768,768]{1,0:T(8,128)(2,1)} %param.47) | copy-start | bytes 3538948
  7.2 7.7 slice-start.10
  7.2 8.2 copy-start.27
  7.2 8.2 copy-start.35
  7.2 8.2 copy-start.37
  7.2 162.8 %all-reduce.14.cloned.1.call-start = ((), (), s32[]{:S(2)}) async-start(), calls=%async_computation.5 | async-start | bytes 12582912 | tf_op jit(solution)/shard_map/psum | solution.py:109
  7.3 8.2 copy-start.7
  11.7 6.1 copy-start.19
  14.7 3.1 copy-start.22
  17.8 7.4 copy-start.16
  18.0 14.3 %copy-start.10 = (bf16[2048,3,64]{0,2,1:T(8,128)(2,1)}, bf16[2048,3,64]{0,2,1:T(8,128)(2,1)S(1)}, u32[]{:S(2)}) copy-start(bf16[2048,3,64]{0,2,1:T(8,128)(2,1)S(1)} %get-tuple-element.179) | copy-start | bytes 2359300
  18.8 2.6 copy-start.8
  20.3 2.6 copy-start.5
  22.9 1.5 copy-start.21
  27.5 3.7 copy-start.4
  36.1 4.6 copy-start.2
  40.7 3.1 copy-start.18
  43.8 126.2 %copy-start.32 = (f32[768]{0:T(1024)S(1)}, f32[768]{0:T(1024)}, u32[]{:S(2)}) copy-start(f32[768]{0:T(1024)} %param.42) | copy-start | bytes 9220
  47.6 267.1 %all-reduce.16.cloned.1.call-start = ((), (), s32[]{:S(2)}) async-start(), calls=%async_computation.6 | async-start | bytes 12582912 | tf_op jit(solution)/shard_map/psum | solution.py:132
  174.7 2.7 copy-start.3
  174.7 0.9 copy-start.24
  174.7 0.9 copy-start.31
  175.6 2.2 copy-start.34
  177.7 2.6 copy-start.14
  177.7 3.0 copy-start.15
  177.7 3.0 copy-start.36
  188.6 1.6 copy-start.40
  194.7 204.4 %all-gather.3.cloned.1.call-start = ((), (), s32[]{:S(2)}) async-start(), calls=%async_computation.10 | async-start | bytes 15728640 | tf_op jit(solution)/shard_map/all_gather | solution.py:12
  201.3 313.3 %reduce-scatter.21.cloned.1.call-start = ((), (), s32[]{:S(2)}) async-start(), calls=%async_computation.13 | async-start | bytes 73728
  202.2 343.6 %reduce-scatter.19.cloned.1.call-start = ((), (), s32[]{:S(2)}) async-start(), calls=%async_computation.12 | async-start | bytes 884736
  399.1 9.0 %copy-start.33 = (f32[768]{0:T(1024)S(1)}, f32[768]{0:T(1024)}, u32[]{:S(2)}) copy-start(f32[768]{0:T(1024)} %param.48) | copy-start | bytes 9220
  418.5 3.5 copy-start.6
  420.8 1.9 copy-start.9
  422.1 3.8 slice-start.6
  423.3 2.5 slice-start.7
  425.9 5.4 slice-start.3
  425.9 5.8 slice-start.4
  430.0 1.9 slice-start.5
  432.0 7.8 slice-start
  432.0 7.8 slice-start.1
  437.7 2.3 slice-start.2
  449.6 2.9 copy-start.11
  449.6 3.7 slice-start.8
  449.6 4.1 slice-start.9
  460.0 5.4 copy-start.17
  476.3 3.2 copy-start.12
  478.4 5.0 copy-start.13
  482.4 133.2 %all-reduce.18.cloned.1.call-start = ((), (), s32[]{:S(2)}) async-start(), calls=%async_computation.7 | async-start | bytes 6291456 | tf_op jit(solution)/shard_map/psum | solution.py:200
  484.8 5.4 copy-start.20
  484.8 5.4 copy-start.23
  484.9 5.4 copy-start.28
  484.9 5.4 copy-start.38
  490.1 196.8 %reduce-scatter.17.cloned.1.call-start = ((), (), s32[]{:S(2)}) async-start(), calls=%async_computation.11 | async-start | bytes 2211840
  498.6 261.1 %reduce-scatter.13.cloned.1.call-start = ((), (), s32[]{:S(2)}) async-start(), calls=%async_computation.8 | async-start | bytes 2654208 | tf_op jit(solution)/shard_map/reduce_scatter | solution.py:213
  505.6 7.1 copy-start.39
  505.6 326.9 %reduce-scatter.15.cloned.1.call-start = ((), (), s32[]{:S(2)}) async-start(), calls=%async_computation.9 | async-start | bytes 2654208 | tf_op jit(solution)/shard_map/reduce_scatter | solution.py:215
  512.6 108.1 %copy-start.25 = (f32[768]{0:T(1024)S(1)}, f32[768]{0:T(1024)}, u32[]{:S(2)}) copy-start(f32[768]{0:T(1024)} %get-tuple-element.154) | copy-start | bytes 9220
  512.6 108.1 %copy-start.26 = (f32[768]{0:T(1024)S(1)}, f32[768]{0:T(1024)}, u32[]{:S(2)}) copy-start(f32[768]{0:T(1024)} %get-tuple-element.159) | copy-start | bytes 9220
  512.6 108.2 %copy-start.29 = (f32[768]{0:T(1024)S(1)}, f32[768]{0:T(1024)}, u32[]{:S(2)}) copy-start(f32[768]{0:T(1024)} %get-tuple-element.173) | copy-start | bytes 9220
  512.6 108.2 %copy-start.30 = (f32[768]{0:T(1024)S(1)}, f32[768]{0:T(1024)}, u32[]{:S(2)}) copy-start(f32[768]{0:T(1024)} %get-tuple-element.181) | copy-start | bytes 9220
  662.4 170.1 %copy-start.1 = (bf16[768,768]{1,0:T(8,128)(2,1)S(1)}, bf16[768,768]{1,0:T(8,128)(2,1)}, u32[]{:S(2)}) copy-start(bf16[768,768]{1,0:T(8,128)(2,1)} %param.47) | copy-start | bytes 3538948
Sparse Core Ops, SparseCore 0:
  47.7 122.2 all-reduce.13
  194.9 119.7 all-reduce.15
  316.8 82.2 all-gather.2
  403.0 62.4 reduce-scatter.20
  482.5 63.2 reduce-scatter.18
  548.0 67.4 all-reduce.17
  619.0 67.8 reduce-scatter.16
  691.0 68.5 reduce-scatter.12
  763.7 68.7 reduce-scatter.14
